TPU v7x, 768 devices: a whole 4x8x12 slice. The times are simulated.
768 devices in a mesh: clu: 96 (over y, z), sub: 8 (over x, core).
Axes of the slice: x: 4, y: 8, z: 12, core: 2. Of those that a mesh axis runs over, the one named last changes fastest.
Arguments:
- operator: bfloat16 [768, 1024, 1024], P(('clu', 'sub')), as said below
- rhs: float32 [768, 1024, 128], P(('clu', 'sub')), may hold values from -6 to 6
- interface_sizes: int32 [768], P(('clu', 'sub')), may hold values from 64 to 1024, as said below
- neighbour_rows: int32 [768, 1024], P(('clu', 'sub')), may hold values from 0 to 1023, each once within a row
- kept_columns: int32 [1, 128], replicated, may hold values 0 or 1
Outputs:
- solution: float32 [768, 1024, 128], P(('clu', 'sub'))
- residual: float32 [768, 1024, 128], P(('clu', 'sub'))
- direction: float32 [768, 1024, 128], P(('clu', 'sub'))
Inputs may be any that keep to these rules, and one draw needn't show every extreme that they name: `operator`: each subdomain's block is symmetric positive definite. `interface_sizes`: some subdomain has all 1024 multipliers live in every draw. `neighbour_rows`: each row is a permutation of 0 to 1023.
All inputs are finite; a program needn't handle non-finite values.
Results may differ from a plain program's by a relative error of at most 0.0065.
Values may be sent and summed in bfloat16 or wider, within the bound.
A program may use at most 32 MiB of HBM per device.

v0:
```python
import functools

import jax
import jax.numpy as jnp
from jax import lax
from jax.sharding import Mesh
from jax.sharding import PartitionSpec as P

CLU = ("clu_0", "clu_1")
CLU_SUB = ("clu_0", "clu_1", "sub")


stiffness = 1.0


def shifted(block, axis, distance):
    devices = range(lax.axis_size(axis))
    route = [(i - distance, i) for i in devices if i - distance in devices]
    return lax.ppermute(block, axis, route)


def sent_to_all(array, axis):
    copies = jnp.broadcast_to(array, (lax.axis_size(axis), *array.shape))
    return lax.all_to_all(copies, axis, split_axis=0, concat_axis=0, tiled=True)


def of_everyone(array, axis):
    return sent_to_all(array, axis).sum(axis=0)


def together(arrays, axis):
    flat, at, done = (jnp.concatenate([a.reshape(-1) for a in arrays]), 0, [])
    subtotal = of_everyone(flat, axis)
    for a in arrays:
        done.append(subtotal[at : at + a.size].reshape(a.shape))
        at += a.size
    return tuple(done)


def over_axes(array, axes):
    return functools.reduce(lax.psum, axes, array)


def of_everyone_2(array, axis):
    everything = sent_to_all(array, axis)
    return jnp.sum(everything.astype(jnp.float32), axis=0)


def three_parts(values):
    upper = values.astype(jnp.bfloat16)
    remainder = values - upper.astype(jnp.float32)
    middle = remainder.astype(jnp.bfloat16)
    lower = (remainder - middle.astype(jnp.float32)).astype(jnp.bfloat16)
    return (upper, middle, lower)


def exact_product(form, narrow, values):
    total = None
    for portion in three_parts(values):
        term = jnp.einsum(form, narrow, portion, preferred_element_type=jnp.float32)
        total = term if total is None else total + term
    return total


def per_device(operator, rhs, interface_sizes, neighbour_rows, kept_columns):
    matrix = operator[0]
    active = interface_sizes[0]
    pairing = neighbour_rows[0]
    height = matrix.shape[0]
    breadth = rhs.shape[2]
    highest = lax.Precision.HIGHEST
    rowmask = (lax.iota(jnp.int32, height) < active).astype(jnp.float32)[:, None]
    inverse = jnp.argsort(pairing)
    position = lax.axis_index(CLU)
    degree = (position > 0).astype(jnp.float32) + (position < lax.axis_size(CLU) - 1).astype(
        jnp.float32
    )
    residual = rhs[0] * rowmask
    direction = residual
    keep = kept_columns[0].astype(jnp.float32)
    rounded = (direction * keep[None, :]).astype(jnp.bfloat16)
    ahead = jnp.take(rounded, inverse, axis=0)
    behind = shifted(rounded, CLU, 1)
    right_rows = shifted(ahead, CLU, -1)
    product = jnp.dot(matrix, rounded, preferred_element_type=jnp.float32)
    left_rows = jnp.take(behind, pairing, axis=0)
    coupling = (
        degree * rounded.astype(jnp.float32)
        - left_rows.astype(jnp.float32)
        - right_rows.astype(jnp.float32)
    )
    image = rowmask * (product + stiffness * coupling)
    joined = exact_product("mk,ml->kl", rounded, jnp.concatenate([image, residual], 1))
    curvature_local = joined[:, :breadth]
    projected_local = joined[:, breadth:]
    grouped = together((curvature_local, projected_local), "sub")
    curvature = over_axes(grouped[0], CLU)
    projected = over_axes(grouped[1], CLU)
    regular = curvature + jnp.diag(1.0 - keep)
    factor = jnp.linalg.cholesky(regular)
    weights = jax.scipy.linalg.cho_solve((factor, True), projected)
    solution = exact_product("mk,kl->ml", rounded, weights)
    residual = residual - jnp.dot(image, weights, precision=highest)
    coupled_local = jnp.einsum("mk,ml->kl", image, residual, precision=highest)
    coupled_group = of_everyone_2(coupled_local.astype(jnp.bfloat16), "sub").astype(jnp.float32)
    coupled = over_axes(coupled_group, CLU)
    correction = jax.scipy.linalg.cho_solve((factor, True), coupled)
    direction = residual - exact_product("mk,kl->ml", rounded, correction)
    return (solution[None], residual[None], direction[None])


def solution(mesh):
    finer = Mesh(mesh.devices.reshape(8, 12, mesh.shape["sub"]), ("clu_0", "clu_1", "sub"))
    in_specs = (P(CLU_SUB, None, None), P(CLU_SUB, None, None), P(CLU_SUB), P(CLU_SUB, None), P())
    out_specs = (P(CLU_SUB, None, None), P(CLU_SUB, None, None), P(CLU_SUB, None, None))
    return jax.shard_map(
        per_device, mesh=finer, in_specs=in_specs, out_specs=out_specs, check_vma=False
    )
```

profile of v0, /device:TPU:1, one launch (start us, length us, event | category | flops | bytes accessed | tf_op | source)
XLA Modules:
  0.0 498.6 jit_solution(17699977040360210768)
XLA Ops:
  8.7 1.2 copy.32
  10.0 5.5 %collective-permute-start = (bf16[1024,128]{0,1:T(8,128)(2,1)S(1)}, bf16[1024,128]{0,1:T(8,128)(2,1)}, u32[]{:S(2)}, u32[]{:S(2)}) collective-permute-start(bf16[1024,128]{0,1:T(8,128)(2,1)S(1)} %get-tuple-element.20), channel_id=1, source_target_pairs={{0,8},{8,16},{16,24},{24,32},{32,40},{40,48},{48,56},{56,64},{64,7... | collective-permute-start | bytes 786440 | tf_op jit(solution)/shard_map/ppermute | solution.py:19
  15.8 4.4 sort.17
  20.1 3.2 gather_fusion.1
  24.2 1.3 collective-permute-start.1
  25.5 2.9 fusion.2
  28.5 1.1 copy.33
  29.6 3.2 gather_fusion
  33.7 1.4 add_multiply_fusion
  36.6 25.0 %all_to_all.11 = f32[8,1,32768]{2,1,0:T(1,128)} all-to-all(f32[8,1,32768]{2,1,0:T(1,128)S(1)} %broadcast_in_dim.46), channel_id=1, replica_groups=mesh['clu_0'=8,'clu_1'=12,'sub'=8] {'sub'}, dimensions={0} | all-to-all | bytes 2097152 | tf_op jit(solution)/shard_map/all_to_all | solution.py:24
  61.6 2.0 reduce_sum.18
  64.5 78.9 %all-reduce.13.cloned.1.call-done = (f32[128,128]{1,0:T(8,128)}, f32[128,128]{1,0:T(8,128)}) async-done(((f32[128,128]{1,0:T(8,128)}, f32[128,128]{1,0:T(8,128)}), (f32[128,128]{1,0:T(8,128)}, f32[128,128]{1,0:T(8,128)})) %all-reduce.13.cloned.1.call-update) | async-done | bytes 131088 | tf_op jit(solution)/shard_map/psum | solution.py:41
  143.4 109.9 %all-reduce.11.cloned.1.call-done = (f32[128,128]{1,0:T(8,128)}, f32[128,128]{1,0:T(8,128)}) async-done(((f32[128,128]{1,0:T(8,128)}, f32[128,128]{1,0:T(8,128)}), (f32[128,128]{1,0:T(8,128)}, f32[128,128]{1,0:T(8,128)})) %all-reduce.11.cloned.1.call-update) | async-done | bytes 131088 | tf_op jit(solution)/shard_map/psum | solution.py:41
  255.3 11.7 %cholesky.19 = f32[128,128]{1,0:T(8,128)S(1)} custom-call(f32[128,128]{1,0:T(8,128)S(1)} %fusion.27), custom_call_target="Cholesky" | custom-call | tf_op jit(solution)/shard_map/jit(cholesky)/cholesky | solution.py:100
  267.7 1.3 fusion.18
  269.0 10.6 %custom-call.9 = f32[1,128,128]{1,2,0:T(8,128)S(1)} custom-call(f32[1,128,128]{2,1,0:T(8,128)} %fusion.18), custom_call_target="InvertDiagBlocksLowerTriangular" | custom-call | tf_op jit(solution)/shard_map/jit(_cho_solve)/triangular_solve | solution.py:101
  279.7 1.1 fusion.25
  283.1 13.2 %all-to-all-start.1 = ((bf16[8,128,128]{2,1,0:T(8,128)(2,1)}), bf16[8,128,128]{2,1,0:T(8,128)(2,1)}, u32[]{:S(2)}, u32[]{:S(2)}) async-start(bf16[8,128,128]{2,1,0:T(8,128)(2,1)} %broadcast_in_dim.51), calls=%async_computation.1 | async-start | bytes 524288 | tf_op jit(solution)/shard_map/all_to_all | solution.py:24
  296.6 6.3 %all-to-all-done.1 = bf16[8,128,128]{2,1,0:T(8,128)(2,1)} async-done(((bf16[8,128,128]{2,1,0:T(8,128)(2,1)}), bf16[8,128,128]{2,1,0:T(8,128)(2,1)}, u32[]{:S(2)}, u32[]{:S(2)}) %all-to-all-start.1) | async-done | bytes 262176 | tf_op jit(solution)/shard_map/all_to_all | solution.py:24
  302.9 1.6 convert_reduce_fusion
  305.7 73.6 %all-reduce.7.cloned.1.call-done = f32[128,128]{1,0:T(8,128)} async-done(((f32[128,128]{1,0:T(8,128)}), f32[128,128]{1,0:T(8,128)}) %all-reduce.7.cloned.1.call-update) | async-done | bytes 65552 | tf_op jit(solution)/shard_map/psum | solution.py:41
  379.3 2.1 fusion.5
  382.4 106.5 %all-reduce.9.cloned.1.call-done = f32[128,128]{1,0:T(8,128)} async-done(((f32[128,128]{1,0:T(8,128)}), f32[128,128]{1,0:T(8,128)}) %all-reduce.9.cloned.1.call-update) | async-done | bytes 65552 | tf_op jit(solution)/shard_map/psum | solution.py:41
  488.9 1.1 fusion.21
  (57 shorter events, 14.5 us)
Async XLA Ops:
  7.2 18.4 %copy-start = (bf16[1,1024,1024]{2,1,0:T(8,128)(2,1)S(1)}, bf16[1,1024,1024]{2,1,0:T(8,128)(2,1)}, u32[]{:S(2)}) copy-start(bf16[1,1024,1024]{2,1,0:T(8,128)(2,1)} %param.9) | copy-start | bytes 6291460
  7.2 8.6 %copy-start.3 = (s32[1,1024]{1,0:T(1,128)S(1)}, s32[1,1024]{1,0:T(1,128)}, u32[]{:S(2)}) copy-start(s32[1,1024]{1,0:T(1,128)} %param.12) | copy-start | bytes 12292
  7.2 136.2 %all-reduce.13.cloned.1.call-start = ((), (), s32[]{:S(2)}) async-start(), calls=%async_computation.5 | async-start | bytes 262144 | tf_op jit(solution)/shard_map/psum | solution.py:41
  10.0 18.4 %collective-permute-start = (bf16[1024,128]{0,1:T(8,128)(2,1)S(1)}, bf16[1024,128]{0,1:T(8,128)(2,1)}, u32[]{:S(2)}, u32[]{:S(2)}) collective-permute-start(bf16[1024,128]{0,1:T(8,128)(2,1)S(1)} %get-tuple-element.20), channel_id=1, source_target_pairs={{0,8},{8,16},{16,24},{24,32},{32,40},{40,48},{48,56},{56,64},{64,7... | collective-permute-start | bytes 786440 | tf_op jit(solution)/shard_map/ppermute | solution.py:19
  24.2 9.4 %collective-permute-start.1 = (bf16[1024,128]{0,1:T(8,128)(2,1)}, bf16[1024,128]{0,1:T(8,128)(2,1)}, u32[]{:S(2)}, u32[]{:S(2)}) collective-permute-start(bf16[1024,128]{0,1:T(8,128)(2,1)} %broadcast_select_fusion), channel_id=1, source_target_pairs={{8,0},{16,8},{24,16},{32,24},{40,32},{48,40},{56,48},{64,56},{72,6... | collective-permute-start | bytes 786440 | tf_op jit(solution)/shard_map/ppermute | solution.py:19
  36.6 106.8 %copy-start.4 = (s32[1,128]{1,0:T(1,128)S(1)}, s32[1,128]{1,0:T(1,128)}, u32[]{:S(2)}) copy-start(s32[1,128]{1,0:T(1,128)} %param.13) | copy-start | bytes 1540
  64.2 189.1 %all-reduce.11.cloned.1.call-start = ((), (), s32[]{:S(2)}) async-start(), calls=%async_computation.4 | async-start | bytes 262144 | tf_op jit(solution)/shard_map/psum | solution.py:41
  281.6 0.8 copy-start.1
  283.1 19.8 %all-to-all-start.1 = ((bf16[8,128,128]{2,1,0:T(8,128)(2,1)}), bf16[8,128,128]{2,1,0:T(8,128)(2,1)}, u32[]{:S(2)}, u32[]{:S(2)}) async-start(bf16[8,128,128]{2,1,0:T(8,128)(2,1)} %broadcast_in_dim.51), calls=%async_computation.1 | async-start | bytes 524288 | tf_op jit(solution)/shard_map/all_to_all | solution.py:24
  296.4 85.1 %copy-start.2 = (f32[1024,128]{0,1:T(8,128)S(1)}, f32[1024,128]{0,1:T(8,128)}, u32[]{:S(2)}) copy-start(f32[1024,128]{0,1:T(8,128)} %copy-done.1) | copy-start | bytes 1572868
  296.4 82.9 %all-reduce.7.cloned.1.call-start = ((), (), s32[]{:S(2)}) async-start(), calls=%async_computation.2 | async-start | bytes 131072 | tf_op jit(solution)/shard_map/psum | solution.py:41
  304.6 184.3 %all-reduce.9.cloned.1.call-start = ((), (), s32[]{:S(2)}) async-start(), calls=%async_computation.3 | async-start | bytes 131072 | tf_op jit(solution)/shard_map/psum | solution.py:41
Sparse Core Ops, SparseCore 0:
  64.4 78.9 all-reduce.12
  145.8 107.5 all-reduce.10
  304.7 74.5 all-reduce.6
  381.5 107.3 all-reduce.8
where the time goes:
time: 506 us; the launch traced here: 499 us
  waiting for transfers between devices  375 us (74%)
  other arithmetic  37 us (7%)
  blocking collectives  25 us (5%)
  starting transfers between devices  20.3 us (4%)
  between operations  14.9 us (3%)
  local copies, waits for them, and re-layouts  14.2 us (3%)
  matrix products  11.9 us (2%)
    psum x4, waiting for transfers between devices, over_axes(): return functools.reduce(lax.psum, axes, array)  369 us
    all_to_all x1, blocking collectives, sent_to_all(): return lax.all_to_all(copies, axis, split_axis=0, concat_axis=0, tiled=True)  25 us
    all_to_all x1, starting transfers between devices, sent_to_all(): return lax.all_to_all(copies, axis, split_axis=0, concat_axis=0, tiled=True)  13.2 us
    another operation x3, other arithmetic, per_device(): factor = jnp.linalg.cholesky(regular)  12.4 us
    another operation x2, other arithmetic, per_device(): weights = jax.scipy.linalg.cho_solve((factor, True), projected)  11.9 us
  transfers between devices with their start and end apart: 7, of which 5 were waited for; matrix products, arithmetic and copies ran while one was open for 4% of the time, Pallas kernels for 0%

commit v1 on v0

v1 whole, which is shorter than its diff:
```python
import functools

import jax
import jax.numpy as jnp
from jax import lax
from jax.experimental import pallas as pl
from jax.experimental.pallas import tpu as pltpu
from jax.sharding import Mesh
from jax.sharding import PartitionSpec as P

AXES = ("y", "z", "x", "core")
F32 = jnp.float32
BF16 = jnp.bfloat16
HIGHEST = lax.Precision.HIGHEST
CHUNKS = 4
stiffness = 1.0


def dot(a, b, contract=((1,), (0,)), precision=None):
    return lax.dot_general(a, b, (contract, ((), ())), precision=precision, preferred_element_type=F32)


def comm_kernel(
    ny, nz, nx, nc,
    op_hbm, rhs_ref, size_ref, nbr_ref, keep_ref,
    image_ref, sums_ref,
    op_ref, pt_ref, rounded_ref, ahead_ref, behind_ref, right_ref,
    gram_ref, xin_ref, ychunk_ref, yin_ref, zown_ref, zin_ref, part_ref,
    op_sem, f_send, f_recv, b_send, b_recv,
    xs, xr, ys, yr, zs, zr, ys2, yr2, xs2, xr2,
):
    y, z, x, core = (lax.axis_index(a) for a in AXES)
    clu = y * nz + z
    nclu = ny * nz
    nsub = nx * nc
    sub = x * nc + core
    nxt = lax.rem(clu + 1, nclu)
    prv = lax.rem(clu + nclu - 1, nclu)

    def at_clu(c):
        return (c // nz, lax.rem(c, nz), x, core)

    def at_sub(s):
        return (y, z, s // nc, lax.rem(s, nc))

    def at_y(v):
        return (v, z, x, core)

    def at_z(v):
        return (y, v, x, core)

    next_id, prev_id = at_clu(nxt), at_clu(prv)
    sub_ids = [None] + [at_sub(lax.rem(sub + d, nsub)) for d in range(1, nsub)]
    y_ids = [None] + [at_y(lax.rem(y + d, ny)) for d in range(1, ny)]
    z_ids = [None] + [at_z(lax.rem(z + d, nz)) for d in range(1, nz)]

    op_copy = pltpu.make_async_copy(op_hbm.at[0], op_ref, op_sem)
    op_copy.start()

    barrier = pltpu.get_barrier_semaphore()
    greeted = [next_id, prev_id] + sub_ids[1:] + y_ids[1:] + z_ids[1:]
    for device in greeted:
        pl.semaphore_signal(barrier, inc=1, device_id=device, device_id_type=pl.DeviceIdType.MESH)

    height, breadth = rounded_ref.shape
    step = height // CHUNKS
    size = size_ref[0]
    keep = keep_ref[...].astype(F32)

    def masked(t):
        rows = lax.broadcasted_iota(jnp.int32, (step, breadth), 0) + t * step
        return jnp.where(rows < size, rhs_ref[0, pl.ds(t * step, step), :], 0.0), rows

    for t in range(CHUNKS):
        live, _ = masked(t)
        rounded_ref[pl.ds(t * step, step), :] = (live * keep).astype(BF16)
        rows = lax.broadcasted_iota(jnp.int32, (step, height), 0) + t * step
        pt_ref[pl.ds(t * step, step), :] = jnp.where(rows == nbr_ref[...], 1.0, 0.0).astype(BF16)
    for t in range(CHUNKS):
        ahead_ref[pl.ds(t * step, step), :] = dot(pt_ref[pl.ds(t * step, step), :], rounded_ref[...]).astype(BF16)

    def remote(src, dst, send, recv, device):
        return pltpu.make_async_remote_copy(
            src_ref=src, dst_ref=dst, send_sem=send, recv_sem=recv,
            device_id=device, device_id_type=pl.DeviceIdType.MESH,
        )

    pl.semaphore_wait(barrier, len(greeted))

    forward, backward = [], []
    for t in range(CHUNKS):
        rows = pl.ds(t * step, step)
        forward.append(remote(rounded_ref.at[rows, :], behind_ref.at[rows, :], f_send.at[t], f_recv.at[t], next_id))
        backward.append(remote(ahead_ref.at[rows, :], right_ref.at[rows, :], b_send.at[t], b_recv.at[t], prev_id))
        forward[t].start()
        backward[t].start()

    has_prev = clu > 0
    has_next = clu < nclu - 1
    degree = has_prev.astype(F32) + has_next.astype(F32)
    op_copy.wait()
    for t in range(CHUNKS):
        rows = pl.ds(t * step, step)
        product = dot(op_ref[rows, :], rounded_ref[...])
        image_ref[rows, :] = product + stiffness * degree * rounded_ref[rows, :].astype(F32)

    prev_scale = jnp.where(has_prev, stiffness, 0.0).astype(F32)
    next_scale = jnp.where(has_next, stiffness, 0.0).astype(F32)
    left_t = None
    for t in range(CHUNKS):
        rows = pl.ds(t * step, step)
        forward[t].wait_recv()
        term = dot(behind_ref[rows, :].astype(F32).T.astype(BF16), pt_ref[rows, :])
        left_t = term if left_t is None else left_t + term
    left = left_t.T
    for t in range(CHUNKS):
        rows = pl.ds(t * step, step)
        backward[t].wait_recv()
        coupled = prev_scale * left[t * step : (t + 1) * step, :] + next_scale * right_ref[rows, :].astype(F32)
        live = lax.broadcasted_iota(jnp.int32, (step, breadth), 0) + t * step < size
        image_ref[rows, :] = jnp.where(live, image_ref[rows, :] - coupled, 0.0)

    gram = None
    for t in range(CHUNKS):
        rows = pl.ds(t * step, step)
        live, _ = masked(t)
        image = image_ref[rows, :]
        lhs = jnp.concatenate([rounded_ref[rows, :].astype(F32), image], axis=1)
        rhs = jnp.concatenate([image, live], axis=1)
        term = dot(lhs, rhs, ((0,), (0,)), HIGHEST)
        gram = term if gram is None else gram + term
    pieces = (
        gram[:breadth, :breadth], gram[:breadth, breadth:],
        gram[breadth:, :breadth], gram[breadth:, breadth:],
    )
    slab = breadth // nsub
    for s in range(nsub):
        for k, piece in enumerate(pieces):
            gram_ref[s, k * slab : (k + 1) * slab, :] = piece[s * slab : (s + 1) * slab, :]

    copies = []
    for d in range(1, nsub):
        peer = lax.rem(sub + d, nsub)
        copies.append(remote(gram_ref.at[peer], xin_ref.at[d], xs.at[d], xr.at[d], sub_ids[d]))
        copies[-1].start()
    total = gram_ref[sub]
    for d in range(1, nsub):
        copies[d - 1].wait_recv()
        total = total + xin_ref[d]
    height_y = total.shape[0] // ny
    for v in range(ny):
        ychunk_ref[v] = total[v * height_y : (v + 1) * height_y, :]

    ycopies = []
    for d in range(1, ny):
        peer = lax.rem(y + d, ny)
        ycopies.append(remote(ychunk_ref.at[peer], yin_ref.at[d], ys.at[d], yr.at[d], y_ids[d]))
        ycopies[-1].start()
    total = ychunk_ref[y]
    for d in range(1, ny):
        ycopies[d - 1].wait_recv()
        total = total + yin_ref[d]
    zown_ref[...] = total

    zcopies = []
    for d in range(1, nz):
        zcopies.append(remote(zown_ref, zin_ref.at[d], zs.at[d], zr.at[d], z_ids[d]))
        zcopies[-1].start()
    for d in range(1, nz):
        zcopies[d - 1].wait_recv()
        total = total + zin_ref[d]
    part_ref[y] = total

    y2 = []
    for d in range(1, ny):
        y2.append(remote(part_ref.at[y], part_ref.at[y], ys2.at[d], yr2.at[d], y_ids[d]))
        y2[-1].start()
    for d in range(1, ny):
        y2[d - 1].wait_recv()
    for v in range(ny):
        sums_ref[sub, v * height_y : (v + 1) * height_y, :] = part_ref[v]
    x2 = []
    for d in range(1, nsub):
        x2.append(remote(sums_ref.at[sub], sums_ref.at[sub], xs2.at[d], xr2.at[d], sub_ids[d]))
        x2[-1].start()
    for d in range(1, nsub):
        x2[d - 1].wait_recv()
    for copy in forward + backward + copies + ycopies + zcopies + y2 + x2:
        copy.wait_send()


def communicate(operator, rhs, sizes, neighbours, kept, ny, nz, nx, nc):
    height, breadth = rhs.shape[1:]
    nsub = nx * nc
    slab = 4 * breadth // nsub
    piece = slab // ny
    vmem = pl.BlockSpec(memory_space=pltpu.VMEM)
    dma = pltpu.SemaphoreType.DMA
    return pl.pallas_call(
        functools.partial(comm_kernel, ny, nz, nx, nc),
        name="exchange_and_sums",
        out_shape=(
            jax.ShapeDtypeStruct((height, breadth), F32),
            jax.ShapeDtypeStruct((nsub, slab, breadth), F32),
        ),
        in_specs=[
            pl.BlockSpec(memory_space=pl.ANY), vmem, pl.BlockSpec(memory_space=pltpu.SMEM), vmem, vmem,
        ],
        out_specs=(vmem, vmem),
        scratch_shapes=[
            pltpu.VMEM((height, height), BF16),
            pltpu.VMEM((height, height), BF16),
            pltpu.VMEM((height, breadth), BF16),
            pltpu.VMEM((height, breadth), BF16),
            pltpu.VMEM((height, breadth), BF16),
            pltpu.VMEM((height, breadth), BF16),
            pltpu.VMEM((nsub, slab, breadth), F32),
            pltpu.VMEM((nsub, slab, breadth), F32),
            pltpu.VMEM((ny, piece, breadth), F32),
            pltpu.VMEM((ny, piece, breadth), F32),
            pltpu.VMEM((piece, breadth), F32),
            pltpu.VMEM((nz, piece, breadth), F32),
            pltpu.VMEM((ny, piece, breadth), F32),
            dma(()),
            dma((CHUNKS,)), dma((CHUNKS,)), dma((CHUNKS,)), dma((CHUNKS,)),
            dma((nsub,)), dma((nsub,)), dma((ny,)), dma((ny,)), dma((nz,)), dma((nz,)),
            dma((ny,)), dma((ny,)), dma((nsub,)), dma((nsub,)),
        ],
        compiler_params=pltpu.CompilerParams(
            collective_id=0, has_side_effects=True, vmem_limit_bytes=48 * 2**20
        ),
    )(operator, rhs, sizes, neighbours, kept)


BLOCK = 8


def three_parts(values):
    upper = values.astype(BF16)
    rest = values - upper.astype(F32)
    middle = rest.astype(BF16)
    lower = (rest - middle.astype(F32)).astype(BF16)
    return upper, middle, lower


def inverse_in_place(ref):
    n = ref.shape[0]
    b = BLOCK
    lane = lax.broadcasted_iota(jnp.int32, (b, n), 1)
    row = lax.broadcasted_iota(jnp.int32, (b, n), 0)
    wide_lane = lax.broadcasted_iota(jnp.int32, (n, n), 1)
    for start in range(0, n, b):
        panel = ref[start : start + b, :]
        columns = [jnp.broadcast_to(panel[:, start + j : start + j + 1], (b, n)) for j in range(b)]
        inside = (lane >= start) & (lane < start + b)
        work = jnp.where(inside, jnp.where(lane - start == row, 1.0, 0.0), panel)
        for j in range(b):
            inv = 1.0 / jnp.broadcast_to(columns[j][j : j + 1, :], (b, n))
            factor = columns[j] * inv
            here = row == j

            def eliminated(value):
                pivot = jnp.broadcast_to(value[j : j + 1, :], (b, n))
                return jnp.where(here, pivot * inv, value - factor * pivot)

            for k in range(j + 1, b):
                columns[k] = eliminated(columns[k])
            work = eliminated(work)
        column = jnp.where(inside, 0.0, jnp.where(lane < start, -panel, panel))
        ch, cm, cl = three_parts(column)
        wh, wm, wl = three_parts(work)
        lhs = jnp.concatenate([ch, ch, cm, cm, ch, cl], axis=0)
        rhs = jnp.concatenate([wh, wm, wh, wm, wl, wh], axis=0)
        update = dot(lhs, rhs, ((0,), (0,)))
        outside = (wide_lane < start) | (wide_lane >= start + b)
        ref[...] = jnp.where(outside, ref[...], 0.0) - update
        ref[start : start + b, :] = work


def solve_kernel(
    size_ref, sums_ref, keep_ref, rhs_ref, image_ref,
    solution_ref, residual_ref, direction_ref,
    inverse_ref, both_ref,
):
    nsub = sums_ref.shape[0]
    slab = sums_ref.shape[1] // 4
    n = inverse_ref.shape[0]
    keep = keep_ref[...].astype(F32)

    @pl.when(pl.program_id(0) == 0)
    def _():
        def matrix(k):
            return jnp.concatenate([sums_ref[s, k * slab : (k + 1) * slab, :] for s in range(nsub)], axis=0)

        curvature = matrix(0)
        rows = lax.broadcasted_iota(jnp.int32, (n, n), 0)
        lanes = lax.broadcasted_iota(jnp.int32, (n, n), 1)
        dropped = jnp.where(rows == lanes, 1.0 - keep, 0.0)
        inverse_ref[...] = 0.5 * (curvature + curvature.T) + dropped
        inverse_in_place(inverse_ref)
        inverse = inverse_ref[...]
        weights = dot(inverse, matrix(1), precision=HIGHEST)
        coupled = matrix(3) - dot(matrix(2), weights, precision=HIGHEST)
        both_ref[:, :n] = weights
        both_ref[:, n:] = dot(inverse, coupled, precision=HIGHEST)

    t, breadth = rhs_ref.shape[1:]
    rows = lax.broadcasted_iota(jnp.int32, (t, breadth), 0) + pl.program_id(0) * t
    live = jnp.where(rows < size_ref[0], rhs_ref[0], 0.0)
    rounded = (live * keep).astype(BF16).astype(F32)
    spread = dot(rounded, both_ref[...], precision=HIGHEST)
    residual = live - dot(image_ref[...], both_ref[:, :n], precision=HIGHEST)
    solution_ref[0] = spread[:, :n]
    residual_ref[0] = residual
    direction_ref[0] = residual - spread[:, n:]


def solve(sizes, sums, kept, rhs, image):
    _, height, breadth = rhs.shape
    tiles = 4
    tile = height // tiles
    whole = pl.BlockSpec((1, tile, breadth), lambda i: (0, i, 0))
    return pl.pallas_call(
        solve_kernel,
        name="solve_and_update",
        grid=(tiles,),
        out_shape=[jax.ShapeDtypeStruct(rhs.shape, F32)] * 3,
        in_specs=[
            pl.BlockSpec(memory_space=pltpu.SMEM),
            pl.BlockSpec(sums.shape, lambda i: (0, 0, 0)),
            pl.BlockSpec((1, breadth), lambda i: (0, 0)),
            whole,
            pl.BlockSpec((tile, breadth), lambda i: (i, 0)),
        ],
        out_specs=[whole] * 3,
        scratch_shapes=[pltpu.VMEM((breadth, breadth), F32), pltpu.VMEM((breadth, 2 * breadth), F32)],
    )(sizes, sums, kept, rhs, image)


def per_device(ny, nz, nx, nc, operator, rhs, interface_sizes, neighbour_rows, kept_columns):
    image, sums = communicate(operator, rhs, interface_sizes, neighbour_rows, kept_columns, ny, nz, nx, nc)
    return tuple(solve(interface_sizes, sums, kept_columns, rhs, image))


def solution(mesh, grid=(8, 12, 4, 2)):
    finer = Mesh(mesh.devices.reshape(grid), AXES)
    in_specs = (P(AXES, None, None), P(AXES, None, None), P(AXES), P(AXES, None), P())
    out_specs = (P(AXES, None, None),) * 3
    return jax.shard_map(
        functools.partial(per_device, *grid), mesh=finer, in_specs=in_specs, out_specs=out_specs, check_vma=False
    )
```

time: 506 us -> 71 us (0.14); the launches traced: 499 us -> 70.6 us
  waiting for transfers between devices: 375 us -> 0 us
  Pallas kernels: 0 us -> 63.9 us
  other arithmetic: 37 us -> 0 us
  blocking collectives: 25 us -> 0 us
  starting transfers between devices: 20.3 us -> 0 us
  between operations: 14.9 us -> 1.31 us
  matrix products: 11.9 us -> 0 us
  local copies, waits for them, and re-layouts: 14.2 us -> 5.45 us
    psum x4 -> x0, waiting for transfers between devices: 369 us -> none  [over_axes(): return functools.reduce(lax.psum, axes, array)]
    pallas_call x0 -> x2, Pallas kernels: none -> 63.9 us  [the longest x1 53.5 us: communicate(): pl.pallas_call(functools.partial(comm_kernel, ny, nz, nx, nc), name='exch...]
    all_to_all x1 -> x0, blocking collectives: 25 us -> none  [sent_to_all(): return lax.all_to_all(copies, axis, split_axis=0, concat_axis=0, tiled=True)]
    another operation x5 -> x0, other arithmetic: 24.3 us -> none  [the longest x3 12.4 us: per_device(): factor = jnp.linalg.cholesky(regular)]
    all_to_all x1 -> x0, starting transfers between devices: 13.2 us -> none  [sent_to_all(): return lax.all_to_all(copies, axis, split_axis=0, concat_axis=0, tiled=True)]
    dot_general x12 -> x0, matrix products: 9.24 us -> none  [the longest x9 5.14 us: exact_product(): term = jnp.einsum(form, narrow, portion, preferred_element_type=jnp.float32)]
    gather x4 -> x0, local copies, waits for them, and re-layouts: 7.41 us -> none  [the longest x2 4.06 us: per_device(): left_rows = jnp.take(behind, pairing, axis=0)]
    ppermute x2 -> x0, starting transfers between devices: 6.8 us -> none  [shifted(): return lax.ppermute(block, axis, route)]
  transfers between devices with their start and end apart: 7 -> 0, of which waited for: 5 -> 0; matrix products, arithmetic and copies ran while one was open for 4% -> 0% of each run, Pallas kernels for 0% -> 0%
where the time goes in v1:
time: 71 us; the launch traced here: 70.6 us
  Pallas kernels  63.9 us (90%)
  local copies, waits for them, and re-layouts  5.45 us (8%)
  between operations  1.31 us (2%)
    pallas_call x1, Pallas kernels, communicate(): pl.pallas_call(functools.partial(comm_kernel, ny, nz, nx, nc), name='exch...  53.5 us
    pallas_call x1, Pallas kernels, solve(): pl.pallas_call(solve_kernel, name='solve_and_update', grid=(tiles,), out_...  10.3 us
    unnamed x12, local copies, waits for them, and re-layouts  5.45 us

profile of v1, /device:TPU:1, one launch (start us, length us, event | category | flops | bytes accessed | tf_op | source)
XLA Modules:
  0.0 70.6 jit_solution(14653023504501896726)
XLA Ops:
  1.3 0.0 copy-start
  1.3 1.0 %copy-done = f32[1,1024,128]{2,1,0:T(8,128)S(1)} copy-done((f32[1,1024,128]{2,1,0:T(8,128)S(1)}, f32[1,1024,128]{2,1,0:T(8,128)}, u32[]{:S(2)}) %copy-start) | copy-done | bytes 524312
  2.3 0.0 copy-start.1
  2.3 1.6 %copy-done.1 = bf16[1,1024,1024]{2,1,0:T(8,128)(2,1)S(1)} copy-done((bf16[1,1024,1024]{2,1,0:T(8,128)(2,1)S(1)}, bf16[1,1024,1024]{2,1,0:T(8,128)(2,1)}, u32[]{:S(2)}) %copy-start.1) | copy-done | bytes 2097176
  3.9 0.0 copy-start.4
  3.9 0.7 copy-done.4
  4.6 0.0 copy-start.5
  4.6 0.7 copy-done.5
  5.3 53.5 %exchange_and_sums.1 = (f32[1024,128]{1,0:T(8,128)S(1)}, f32[8,64,128]{2,1,0:T(8,128)S(1)}) custom-call(bf16[1,1024,1024]{2,1,0:T(8,128)(2,1)S(1)} %copy-done.1, f32[1,1024,128]{2,1,0:T(8,128)S(1)} %copy-done, s32[1]{0:T(128)S(6)} %copy.8.size_ref, s32[1,1024]{1,0:T(1,128)S(1)} %copy-done.4, s32[1,128]{1,0:T(1,128)S(1)} %copy-done.5), custom_call_target="tpu_custom_call" | custom-call | tf_op jit(solution)/shard_map/exchange_and_sums/pallas_call | solution.py:199
  58.8 0.0 copy-start.2
  58.8 0.8 %copy-done.2 = f32[1024,128]{1,0:T(8,128)} copy-done((f32[1024,128]{1,0:T(8,128)}, f32[1024,128]{1,0:T(8,128)S(1)}, u32[]{:S(2)}) %copy-start.2) | copy-done | bytes 524312
  59.6 0.0 copy-start.3
  59.6 0.7 copy-done.3
  60.3 10.3 %solve_and_update.1 = (f32[1,1024,128]{2,1,0:T(8,128)}, f32[1,1024,128]{2,1,0:T(8,128)}, f32[1,1024,128]{2,1,0:T(8,128)}) custom-call(s32[1]{0:T(128)S(6)} %copy.8.size_ref, f32[8,64,128]{2,1,0:T(8,128)} %copy-done.3, s32[1,128]{1,0:T(1,128)} %keep_ref.3, f32[1,1024,128]{2,1,0:T(8,128)} %rhs_ref.3, f32[1024,128]{1,0:T(8,128)} %copy-done.2), custom_call_target="tpu_custom_call" | custom-call | tf_op jit(solution)/shard_map/solve_and_update/pallas_call | solution.py:323
Async XLA Ops:
  1.3 1.0 %copy-start = (f32[1,1024,128]{2,1,0:T(8,128)S(1)}, f32[1,1024,128]{2,1,0:T(8,128)}, u32[]{:S(2)}) copy-start(f32[1,1024,128]{2,1,0:T(8,128)} %rhs_ref.3) | copy-start | bytes 1572868
  2.3 1.6 %copy-start.1 = (bf16[1,1024,1024]{2,1,0:T(8,128)(2,1)S(1)}, bf16[1,1024,1024]{2,1,0:T(8,128)(2,1)}, u32[]{:S(2)}) copy-start(bf16[1,1024,1024]{2,1,0:T(8,128)(2,1)} %op_hbm.1) | copy-start | bytes 6291460
  3.9 0.7 copy-start.4
  4.6 0.7 copy-start.5
  58.8 0.8 %copy-start.2 = (f32[1024,128]{1,0:T(8,128)}, f32[1024,128]{1,0:T(8,128)S(1)}, u32[]{:S(2)}) copy-start(f32[1024,128]{1,0:T(8,128)S(1)} %get-tuple-element.6.image_ref) | copy-start | bytes 1572868
  59.6 0.7 copy-start.3

commit v2 on v0

v2 whole, which is shorter than its diff:
```python
import functools

import jax
import jax.numpy as jnp
from jax import lax
from jax.experimental import pallas as pl
from jax.experimental.pallas import tpu as pltpu
from jax.sharding import Mesh
from jax.sharding import PartitionSpec as P

AXES = ("y", "z", "x", "core")
F32 = jnp.float32
BF16 = jnp.bfloat16
HIGHEST = lax.Precision.HIGHEST
CHUNKS = 4
stiffness = 1.0


def dot(a, b, contract=((1,), (0,)), precision=None):
    return lax.dot_general(a, b, (contract, ((), ())), precision=precision, preferred_element_type=F32)


def three_parts(values):
    upper = values.astype(BF16)
    rest = values - upper.astype(F32)
    middle = rest.astype(BF16)
    lower = (rest - middle.astype(F32)).astype(BF16)
    return upper, middle, lower


def two_parts(values):
    upper = values.astype(BF16)
    return upper, (values - upper.astype(F32)).astype(BF16)


def sweep_block(k, ref):
    n = ref.shape[0]
    b = BLOCK
    start = pl.multiple_of(k * b, b)
    lane = lax.broadcasted_iota(jnp.int32, (b, n), 1)
    row = lax.broadcasted_iota(jnp.int32, (b, n), 0)
    wide_lane = lax.broadcasted_iota(jnp.int32, (n, n), 1)
    panel = ref[pl.ds(start, b), :]
    turned = pltpu.roll(panel, lax.rem(n - start, n), axis=1)
    columns = [jnp.broadcast_to(turned[:, j : j + 1], (b, n)) for j in range(b)]
    inside = (lane >= start) & (lane < start + b)
    work = jnp.where(inside, jnp.where(lane - start == row, 1.0, 0.0), panel)
    for j in range(b):
        inv = 1.0 / jnp.broadcast_to(columns[j][j : j + 1, :], (b, n))
        factor = columns[j] * inv
        here = row == j

        def eliminated(value):
            pivot = jnp.broadcast_to(value[j : j + 1, :], (b, n))
            return jnp.where(here, pivot * inv, value - factor * pivot)

        for i in range(j + 1, b):
            columns[i] = eliminated(columns[i])
        work = eliminated(work)
    column = jnp.where(inside, 0.0, jnp.where(lane < start, -panel, panel))
    ch, cm, cl = three_parts(column)
    wh, wm, wl = three_parts(work)
    lhs = jnp.concatenate([ch, ch, cm, cm, ch, cl], axis=0)
    rhs = jnp.concatenate([wh, wm, wh, wm, wl, wh], axis=0)
    update = dot(lhs, rhs, ((0,), (0,)))
    outside = (wide_lane < start) | (wide_lane >= start + b)
    ref[...] = jnp.where(outside, ref[...], 0.0) - update
    ref[pl.ds(start, b), :] = work


def comm_kernel(
    ny, nz, nx, nc,
    op_hbm, rhs_hbm, size_ref, nbr_hbm, keep_hbm,
    live_ref, image_ref, inverse_ref, rest_ref,
    op_ref, pt_ref, pm_ref, rounded_ref, ahead_ref, behind_ref, right_ref, nbr_ref, keep_ref,
    cgram_ref, cxin_ref, cy_ref, cyin_ref, cz_ref, czin_ref, csum_ref,
    gram_ref, xin_ref, ychunk_ref, yin_ref, zown_ref, zin_ref, part_ref,
    in_sem, f_send, f_recv, b_send, b_recv,
    cxs, cxr, cys, cyr, czs, czr, cxs2, cxr2,
    xs, xr, ys, yr, zs, zr, ys2, yr2, xs2, xr2,
):
    y, z, x, core = (lax.axis_index(a) for a in AXES)
    clu = y * nz + z
    nclu = ny * nz
    nsub = nx * nc
    sub = x * nc + core
    nxt = lax.rem(clu + 1, nclu)
    prv = lax.rem(clu + nclu - 1, nclu)

    def at_clu(c):
        return (c // nz, lax.rem(c, nz), x, core)

    def at_sub(s):
        return (y, z, s // nc, lax.rem(s, nc))

    next_id, prev_id = at_clu(nxt), at_clu(prv)
    sub_ids = [None] + [at_sub(lax.rem(sub + d, nsub)) for d in range(1, nsub)]
    y_ids = [None] + [(lax.rem(y + d, ny), z, x, core) for d in range(1, ny)]
    z_ids = [None] + [(y, lax.rem(z + d, nz), x, core) for d in range(1, nz)]

    barrier = pltpu.get_barrier_semaphore()
    greeted = [next_id, prev_id] + sub_ids[1:] + y_ids[1:] + z_ids[1:]
    for device in greeted:
        pl.semaphore_signal(barrier, inc=1, device_id=device, device_id_type=pl.DeviceIdType.MESH)

    loads = [
        pltpu.make_async_copy(src, dst, in_sem.at[i])
        for i, (src, dst) in enumerate(
            [(rhs_hbm.at[0], live_ref), (keep_hbm, keep_ref), (nbr_hbm, nbr_ref), (op_hbm.at[0], op_ref)]
        )
    ]
    for load in loads:
        load.start()

    height, breadth = rounded_ref.shape
    step = height // CHUNKS
    size = size_ref[0]
    tiles = [pl.ds(t * step, step) for t in range(CHUNKS)]

    def remote(src, dst, send, recv, device):
        return pltpu.make_async_remote_copy(
            src_ref=src, dst_ref=dst, send_sem=send, recv_sem=recv,
            device_id=device, device_id_type=pl.DeviceIdType.MESH,
        )

    for load in loads[:3]:
        load.wait()
    keep = keep_ref[...].astype(F32)
    for t, rows in enumerate(tiles):
        index = lax.broadcasted_iota(jnp.int32, (step, breadth), 0) + t * step
        live = jnp.where(index < size, live_ref[rows, :], 0.0)
        live_ref[rows, :] = live
        rounded_ref[rows, :] = (live * keep).astype(BF16)
        index = lax.broadcasted_iota(jnp.int32, (step, height), 0) + t * step
        pt_ref[rows, :] = jnp.where(index == nbr_ref[...], 1.0, 0.0).astype(BF16)
    for rows in tiles:
        ahead_ref[rows, :] = dot(pt_ref[rows, :], rounded_ref[...]).astype(BF16)

    pl.semaphore_wait(barrier, len(greeted))

    forward, backward = [], []
    for t, rows in enumerate(tiles):
        forward.append(remote(rounded_ref.at[rows, :], behind_ref.at[rows, :], f_send.at[t], f_recv.at[t], next_id))
        backward.append(remote(ahead_ref.at[rows, :], right_ref.at[rows, :], b_send.at[t], b_recv.at[t], prev_id))
        forward[t].start()
        backward[t].start()

    tall = jnp.broadcast_to(nbr_ref[...].astype(F32), (breadth, height)).T
    for c in range(0, height, breadth):
        lanes = (lax.broadcasted_iota(jnp.int32, (height, breadth), 1) + c).astype(F32)
        pm_ref[:, c : c + breadth] = jnp.where(tall == lanes, 1.0, 0.0).astype(BF16)
    has_prev = clu > 0
    has_next = clu < nclu - 1
    degree = has_prev.astype(F32) + has_next.astype(F32)
    loads[3].wait()
    for rows in tiles:
        product = dot(op_ref[rows, :], rounded_ref[...])
        image_ref[rows, :] = product + stiffness * degree * rounded_ref[rows, :].astype(F32)

    prev_scale = jnp.where(has_prev, stiffness, 0.0).astype(F32)
    next_scale = jnp.where(has_next, stiffness, 0.0).astype(F32)
    for t, rows in enumerate(tiles):
        backward[t].wait_recv()
        image_ref[rows, :] = image_ref[rows, :] - next_scale * right_ref[rows, :].astype(F32)
        forward[t].wait_recv()
        if t < CHUNKS - 1:
            block = behind_ref[rows, :]
            for out in tiles:
                left = dot(pm_ref[out, rows], block)
                image_ref[out, :] = image_ref[out, :] - prev_scale * left
    block = behind_ref[tiles[-1], :]
    gram = None
    for t, out in enumerate(tiles):
        left = dot(pm_ref[out, tiles[-1]], block)
        index = lax.broadcasted_iota(jnp.int32, (step, breadth), 0) + t * step
        image = jnp.where(index < size, image_ref[out, :] - prev_scale * left, 0.0)
        image_ref[out, :] = image
        lhs = jnp.concatenate([rounded_ref[out, :].astype(F32), image], axis=1)
        rhs = jnp.concatenate([image, live_ref[out, :]], axis=1)
        term = dot(lhs, rhs, ((0,), (0,)), HIGHEST)
        gram = term if gram is None else gram + term
    curvature = gram[:breadth, :breadth]
    others = (gram[:breadth, breadth:], gram[breadth:, :breadth], gram[breadth:, breadth:])
    slab = breadth // nsub
    for s in range(nsub):
        cgram_ref[s] = curvature[s * slab : (s + 1) * slab, :]

    sent = forward + backward

    def scatter(source, place, count, landing, send, recv, ids):
        copies = []
        for d in range(1, count):
            peer = lax.rem(place + d, count)
            copies.append(remote(source.at[peer], landing.at[d], send.at[d], recv.at[d], ids[d]))
            copies[-1].start()
        sent.extend(copies)
        return copies

    def spread(source, count, landing, send, recv, ids):
        copies = []
        for d in range(1, count):
            copies.append(remote(source, landing.at[d], send.at[d], recv.at[d], ids[d]))
            copies[-1].start()
        sent.extend(copies)
        return copies

    def share(array, place, count, send, recv, ids):
        copies = []
        for d in range(1, count):
            copies.append(remote(array.at[place], array.at[place], send.at[d], recv.at[d], ids[d]))
            copies[-1].start()
        sent.extend(copies)
        return copies

    def add_up(total, copies, landing):
        for d, copy in enumerate(copies, 1):
            copy.wait_recv()
            total = total + landing[d]
        return total

    cx = scatter(cgram_ref, sub, nsub, cxin_ref, cxs, cxr, sub_ids)
    for s in range(nsub):
        for k, piece in enumerate(others):
            gram_ref[s, k * slab : (k + 1) * slab, :] = piece[s * slab : (s + 1) * slab, :]
    rx = scatter(gram_ref, sub, nsub, xin_ref, xs, xr, sub_ids)

    cy_ref[...] = add_up(cgram_ref[sub], cx, cxin_ref)
    cy = spread(cy_ref, ny, cyin_ref, cys, cyr, y_ids)
    total = add_up(gram_ref[sub], rx, xin_ref)
    rows_y = total.shape[0] // ny
    for v in range(ny):
        ychunk_ref[v] = total[v * rows_y : (v + 1) * rows_y, :]
    ry = scatter(ychunk_ref, y, ny, yin_ref, ys, yr, y_ids)

    cz_ref[...] = add_up(cy_ref[...], cy, cyin_ref)
    cz = spread(cz_ref, nz, czin_ref, czs, czr, z_ids)
    zown_ref[...] = add_up(ychunk_ref[y], ry, yin_ref)
    rz = spread(zown_ref, nz, zin_ref, zs, zr, z_ids)

    csum_ref[sub] = add_up(cz_ref[...], cz, czin_ref)
    cx2 = share(csum_ref, sub, nsub, cxs2, cxr2, sub_ids)
    part_ref[y] = add_up(zown_ref[...], rz, zin_ref)
    ry2 = share(part_ref, y, ny, ys2, yr2, y_ids)

    for copy in cx2:
        copy.wait_recv()
    summed = jnp.concatenate([csum_ref[s] for s in range(nsub)], axis=0)
    rows = lax.broadcasted_iota(jnp.int32, (breadth, breadth), 0)
    lanes = lax.broadcasted_iota(jnp.int32, (breadth, breadth), 1)
    inverse_ref[...] = 0.5 * (summed + summed.T) + jnp.where(rows == lanes, 1.0 - keep, 0.0)

    def sweep(first, last):
        def one(k, carry):
            sweep_block(k, inverse_ref)
            return carry

        lax.fori_loop(first, last, one, 0)

    blocks = breadth // BLOCK
    sweep(0, blocks // 4)
    for copy in ry2:
        copy.wait_recv()
    for v in range(ny):
        rest_ref[sub, v * rows_y : (v + 1) * rows_y, :] = part_ref[v]
    rx2 = share(rest_ref, sub, nsub, xs2, xr2, sub_ids)
    sweep(blocks // 4, blocks)
    for copy in rx2:
        copy.wait_recv()
    for copy in sent:
        copy.wait_send()


def communicate(operator, rhs, sizes, neighbours, kept, ny, nz, nx, nc):
    height, breadth = rhs.shape[1:]
    nsub = nx * nc
    slab = breadth // nsub
    piece = 3 * slab // ny
    vmem = pl.BlockSpec(memory_space=pltpu.VMEM)
    hbm = pl.BlockSpec(memory_space=pltpu.HBM)
    dma = pltpu.SemaphoreType.DMA
    tall = (height, breadth)
    return pl.pallas_call(
        functools.partial(comm_kernel, ny, nz, nx, nc),
        name="exchange_and_sums",
        out_shape=(
            jax.ShapeDtypeStruct(tall, F32),
            jax.ShapeDtypeStruct(tall, F32),
            jax.ShapeDtypeStruct((breadth, breadth), F32),
            jax.ShapeDtypeStruct((nsub, 3 * slab, breadth), F32),
        ),
        in_specs=[hbm, hbm, pl.BlockSpec(memory_space=pltpu.SMEM), hbm, hbm],
        out_specs=(vmem,) * 4,
        scratch_shapes=[
            pltpu.VMEM((height, height), BF16),
            pltpu.VMEM((height, height), BF16),
            pltpu.VMEM((height, height), BF16),
            pltpu.VMEM(tall, BF16),
            pltpu.VMEM(tall, BF16),
            pltpu.VMEM(tall, BF16),
            pltpu.VMEM(tall, BF16),
            pltpu.VMEM((1, height), jnp.int32),
            pltpu.VMEM((1, breadth), jnp.int32),
            pltpu.VMEM((nsub, slab, breadth), F32),
            pltpu.VMEM((nsub, slab, breadth), F32),
            pltpu.VMEM((slab, breadth), F32),
            pltpu.VMEM((ny, slab, breadth), F32),
            pltpu.VMEM((slab, breadth), F32),
            pltpu.VMEM((nz, slab, breadth), F32),
            pltpu.VMEM((nsub, slab, breadth), F32),
            pltpu.VMEM((nsub, 3 * slab, breadth), F32),
            pltpu.VMEM((nsub, 3 * slab, breadth), F32),
            pltpu.VMEM((ny, piece, breadth), F32),
            pltpu.VMEM((ny, piece, breadth), F32),
            pltpu.VMEM((piece, breadth), F32),
            pltpu.VMEM((nz, piece, breadth), F32),
            pltpu.VMEM((ny, piece, breadth), F32),
            dma((4,)),
            dma((CHUNKS,)), dma((CHUNKS,)), dma((CHUNKS,)), dma((CHUNKS,)),
            dma((nsub,)), dma((nsub,)), dma((ny,)), dma((ny,)), dma((nz,)), dma((nz,)), dma((nsub,)), dma((nsub,)),
            dma((nsub,)), dma((nsub,)), dma((ny,)), dma((ny,)), dma((nz,)), dma((nz,)),
            dma((ny,)), dma((ny,)), dma((nsub,)), dma((nsub,)),
        ],
        compiler_params=pltpu.CompilerParams(
            collective_id=0, has_side_effects=True, vmem_limit_bytes=55230000
        ),
    )(operator, rhs, sizes, neighbours, kept)


BLOCK = 8


def update_kernel(
    live_ref, image_ref, inverse_ref, rest_ref, keep_ref,
    solution_hbm, residual_hbm, direction_hbm,
    solution_ref, residual_ref, direction_ref, sems,
):
    nsub, rows3 = rest_ref.shape[:2]
    slab = rows3 // 3
    keep = keep_ref[...].astype(F32)
    height = live_ref.shape[0]
    step = height // CHUNKS

    def matrix(k):
        return jnp.concatenate([rest_ref[s, k * slab : (k + 1) * slab, :] for s in range(nsub)], axis=0)

    inverse = inverse_ref[...]
    weights = dot(inverse, matrix(0), precision=HIGHEST)
    coupled = matrix(2) - dot(matrix(1), weights, precision=HIGHEST)
    correction = dot(inverse, coupled, precision=HIGHEST)
    wh, wm, wl = three_parts(weights)
    zh, zm, zl = three_parts(correction)
    n = weights.shape[0]
    wide = jnp.concatenate([wh, wm, wl, zh, zm, zl], axis=1)
    copies = []
    for t in range(CHUNKS):
        rows = pl.ds(t * step, step)
        live = live_ref[rows, :]
        rounded = (live * keep).astype(BF16)
        spread = dot(rounded, wide)
        ih, im, il = three_parts(image_ref[rows, :])
        first = dot(ih, wide[:, : 3 * n])
        second = dot(im, wide[:, : 2 * n])
        third = dot(il, wh)
        moved = first[:, :n] + (first[:, n : 2 * n] + second[:, :n]) + (first[:, 2 * n :] + second[:, n:] + third)
        residual = live - moved
        solution_ref[rows, :] = spread[:, :n] + spread[:, n : 2 * n] + spread[:, 2 * n : 3 * n]
        residual_ref[rows, :] = residual
        direction_ref[rows, :] = residual - (
            spread[:, 3 * n : 4 * n] + spread[:, 4 * n : 5 * n] + spread[:, 5 * n :]
        )
        for k, (src, dst) in enumerate(
            [(solution_ref, solution_hbm), (residual_ref, residual_hbm), (direction_ref, direction_hbm)]
        ):
            copies.append(pltpu.make_async_copy(src.at[rows, :], dst.at[0, rows, :], sems.at[k, t]))
            copies[-1].start()
    for copy in copies:
        copy.wait()


def update(live, image, inverse, rest, kept):
    vmem = pl.BlockSpec(memory_space=pltpu.VMEM)
    return pl.pallas_call(
        update_kernel,
        name="update",
        out_shape=[jax.ShapeDtypeStruct((1, *live.shape), F32)] * 3,
        in_specs=[vmem] * 5,
        out_specs=[pl.BlockSpec(memory_space=pltpu.HBM)] * 3,
        scratch_shapes=[pltpu.VMEM(live.shape, F32)] * 3 + [pltpu.SemaphoreType.DMA((3, CHUNKS))],
        compiler_params=pltpu.CompilerParams(vmem_limit_bytes=40 * 2**20),
    )(live, image, inverse, rest, kept)


def per_device(ny, nz, nx, nc, operator, rhs, interface_sizes, neighbour_rows, kept_columns):
    results = communicate(operator, rhs, interface_sizes, neighbour_rows, kept_columns, ny, nz, nx, nc)
    return tuple(update(*results, kept_columns))


def solution(mesh, grid=(8, 12, 4, 2)):
    finer = Mesh(mesh.devices.reshape(grid), AXES)
    in_specs = (P(AXES, None, None), P(AXES, None, None), P(AXES), P(AXES, None), P())
    out_specs = (P(AXES, None, None),) * 3
    return jax.shard_map(
        functools.partial(per_device, *grid), mesh=finer, in_specs=in_specs, out_specs=out_specs, check_vma=False
    )
```

time: 506 us -> 63.3 us (0.13); the launches traced: 499 us -> 63.1 us
  waiting for transfers between devices: 375 us -> 0 us
  Pallas kernels: 0 us -> 60.4 us
  other arithmetic: 37 us -> 0 us
  blocking collectives: 25 us -> 0 us
  starting transfers between devices: 20.3 us -> 0 us
  between operations: 14.9 us -> 1.29 us
  local copies, waits for them, and re-layouts: 14.2 us -> 1.33 us
  matrix products: 11.9 us -> 0 us
    psum x4 -> x0, waiting for transfers between devices: 369 us -> none  [over_axes(): return functools.reduce(lax.psum, axes, array)]
    pallas_call x0 -> x2, Pallas kernels: none -> 60.4 us  [the longest x1 58 us: communicate(): pl.pallas_call(functools.partial(comm_kernel, ny, nz, nx, nc), name='exch...]
    all_to_all x1 -> x0, blocking collectives: 25 us -> none  [sent_to_all(): return lax.all_to_all(copies, axis, split_axis=0, concat_axis=0, tiled=True)]
    another operation x5 -> x0, other arithmetic: 24.3 us -> none  [the longest x3 12.4 us: per_device(): factor = jnp.linalg.cholesky(regular)]
    all_to_all x1 -> x0, starting transfers between devices: 13.2 us -> none  [sent_to_all(): return lax.all_to_all(copies, axis, split_axis=0, concat_axis=0, tiled=True)]
    dot_general x12 -> x0, matrix products: 9.24 us -> none  [the longest x9 5.14 us: exact_product(): term = jnp.einsum(form, narrow, portion, preferred_element_type=jnp.float32)]
    gather x4 -> x0, local copies, waits for them, and re-layouts: 7.41 us -> none  [the longest x2 4.06 us: per_device(): left_rows = jnp.take(behind, pairing, axis=0)]
    ppermute x2 -> x0, starting transfers between devices: 6.8 us -> none  [shifted(): return lax.ppermute(block, axis, route)]
  transfers between devices with their start and end apart: 7 -> 0, of which waited for: 5 -> 0; matrix products, arithmetic and copies ran while one was open for 4% -> 0% of each run, Pallas kernels for 0% -> 0%
where the time goes in v2:
time: 63.3 us; the launch traced here: 63.1 us
  Pallas kernels  60.4 us (95%)
  local copies, waits for them, and re-layouts  1.33 us (2%)
  between operations  1.29 us (2%)
    pallas_call x1, Pallas kernels, communicate(): pl.pallas_call(functools.partial(comm_kernel, ny, nz, nx, nc), name='exch...  58 us
    pallas_call x1, Pallas kernels, update(): pl.pallas_call(update_kernel, name='update', out_shape=[jax.ShapeDtypeStr...  2.43 us
    unnamed x4, local copies, waits for them, and re-layouts  1.33 us

profile of v2, /device:TPU:1, one launch (start us, length us, event | category | flops | bytes accessed | tf_op | source)
XLA Modules:
  0.0 63.1 jit_solution(9408033046273861070)
XLA Ops:
  1.3 0.0 copy-start
  1.3 0.7 %copy-done = s32[1,1024]{1,0:T(1,128)S(1)} copy-done((s32[1,1024]{1,0:T(1,128)S(1)}, s32[1,1024]{1,0:T(1,128)}, u32[]{:S(2)}) %copy-start) | copy-done | bytes 4120
  2.0 0.0 copy-start.1
  2.0 0.7 %copy-done.1 = s32[1,128]{1,0:T(1,128)S(1)} copy-done((s32[1,128]{1,0:T(1,128)S(1)}, s32[1,128]{1,0:T(1,128)}, u32[]{:S(2)}) %copy-start.1) | copy-done | bytes 536
  2.6 58.0 %exchange_and_sums.1 = (f32[1024,128]{1,0:T(8,128)S(1)}, f32[1024,128]{1,0:T(8,128)S(1)}, f32[128,128]{1,0:T(8,128)S(1)}, f32[8,48,128]{2,1,0:T(8,128)S(1)}) custom-call(bf16[1,1024,1024]{2,1,0:T(8,128)(2,1)} %op_hbm.1, f32[1,1024,128]{2,1,0:T(8,128)} %rhs_hbm.1, s32[1]{0:T(128)S(6)} %copy.8.size_ref, s32[1,1024]{1,0:T(1,128)S(1)} %copy-done, ...), custom_call_target="tpu_custom_call" | custom-call | tf_op jit(solution)/shard_map/exchange_and_sums/pallas_call | solution.py:282
  60.6 2.4 %update.1 = (f32[1,1024,128]{2,1,0:T(8,128)}, f32[1,1024,128]{2,1,0:T(8,128)}, f32[1,1024,128]{2,1,0:T(8,128)}) custom-call(f32[1024,128]{1,0:T(8,128)S(1)} %get-tuple-element.7.live_ref, f32[1024,128]{1,0:T(8,128)S(1)} %get-tuple-element.8.image_ref, f32[128,128]{1,0:T(8,128)S(1)} %get-tuple-element.9.inverse_ref, ...), custom_call_target="tpu_custom_call" | custom-call | tf_op jit(solution)/shard_map/update/pallas_call | solution.py:382
Async XLA Ops:
  1.3 0.7 %copy-start = (s32[1,1024]{1,0:T(1,128)S(1)}, s32[1,1024]{1,0:T(1,128)}, u32[]{:S(2)}) copy-start(s32[1,1024]{1,0:T(1,128)} %nbr_hbm.1) | copy-start | bytes 12292
  2.0 0.7 %copy-start.1 = (s32[1,128]{1,0:T(1,128)S(1)}, s32[1,128]{1,0:T(1,128)}, u32[]{:S(2)}) copy-start(s32[1,128]{1,0:T(1,128)} %keep_ref.1) | copy-start | bytes 1540

commit v3 on v2

--- a/solution.py
+++ b/solution.py
@@ -68,14 +68,44 @@
     ref[pl.ds(start, b), :] = work
 
 
+def pack(matrix, ref):
+    n = matrix.shape[0]
+    half, count = n // 2, ref.shape[0]
+    each = half // count
+    matrix = 0.5 * (matrix + matrix.T)
+    row = lax.broadcasted_iota(jnp.int32, (half, n), 0)
+    lane = lax.broadcasted_iota(jnp.int32, (half, n), 1)
+    upper = matrix[:half, :]
+    turned = pltpu.roll(matrix[half:, :], half, axis=1)
+    packed = jnp.where((lane < half) & (lane > row), turned, upper)
+    diagonal = jnp.sum(jnp.where(lane == row, turned, 0.0), axis=0, keepdims=True)
+    for s in range(count):
+        ref[s, :each, :] = packed[s * each : (s + 1) * each, :]
+        ref[s, each : each + 1, :] = diagonal
+
+
+def unpack(ref):
+    count, each, n = ref.shape
+    each, half = each - 1, n // 2
+    packed = jnp.concatenate([ref[s, :each, :] for s in range(count)], axis=0)
+    diagonal = ref[0, each : each + 1, :]
+    row = lax.broadcasted_iota(jnp.int32, (half, n), 0)
+    lane = lax.broadcasted_iota(jnp.int32, (half, n), 1)
+    turned = jnp.concatenate([packed, packed], axis=0).T
+    upper = jnp.where((lane < half) & (lane > row), turned[:half, :], packed)
+    lower = jnp.where(lane > row, packed, jnp.where(lane == row, diagonal, turned[:half, :]))
+    lower = jnp.where(lane < half, turned[half:, :], pltpu.roll(lower, half, axis=1))
+    return jnp.concatenate([upper, lower], axis=0)
+
+
 def comm_kernel(
     ny, nz, nx, nc,
     op_hbm, rhs_hbm, size_ref, nbr_hbm, keep_hbm,
-    live_ref, image_ref, inverse_ref, rest_ref,
-    op_ref, pt_ref, pm_ref, rounded_ref, ahead_ref, behind_ref, right_ref, nbr_ref, keep_ref,
+    live_ref, rounded_ref, image_ref, inverse_ref, rest_ref,
+    op_ref, pt_ref, pm_ref, ahead_ref, behind_ref, right_ref, nbr_ref, keep_ref,
     cgram_ref, cxin_ref, cy_ref, cyin_ref, cz_ref, czin_ref, csum_ref,
     gram_ref, xin_ref, ychunk_ref, yin_ref, zown_ref, zin_ref, part_ref,
-    in_sem, f_send, f_recv, b_send, b_recv,
+    y_known, z_known, in_sem, f_send, f_recv, b_send, b_recv,
     cxs, cxr, cys, cyr, czs, czr, cxs2, cxr2,
     xs, xr, ys, yr, zs, zr, ys2, yr2, xs2, xr2,
 ):
@@ -99,9 +129,13 @@
     z_ids = [None] + [(y, lax.rem(z + d, nz), x, core) for d in range(1, nz)]
 
     barrier = pltpu.get_barrier_semaphore()
-    greeted = [next_id, prev_id] + sub_ids[1:] + y_ids[1:] + z_ids[1:]
+    greeted = [next_id, prev_id, y_ids[1], y_ids[-1], z_ids[1], z_ids[-1]] + sub_ids[1:]
+
+    def signal(semaphore, device):
+        pl.semaphore_signal(semaphore, inc=1, device_id=device, device_id_type=pl.DeviceIdType.MESH)
+
     for device in greeted:
-        pl.semaphore_signal(barrier, inc=1, device_id=device, device_id_type=pl.DeviceIdType.MESH)
+        signal(barrier, device)
 
     loads = [
         pltpu.make_async_copy(src, dst, in_sem.at[i])
@@ -157,6 +191,15 @@
         product = dot(op_ref[rows, :], rounded_ref[...])
         image_ref[rows, :] = product + stiffness * degree * rounded_ref[rows, :].astype(F32)
 
+    for r in range(max(ny, nz) // 2 - 1):
+        rings = [(known, ids) for known, ids, n in ((y_known, y_ids, ny), (z_known, z_ids, nz)) if r < n // 2 - 1]
+        for known, ids in rings:
+            signal(known.at[2 * r], ids[1])
+            signal(known.at[2 * r + 1], ids[-1])
+        for known, ids in rings:
+            pl.semaphore_wait(known.at[2 * r], 1)
+            pl.semaphore_wait(known.at[2 * r + 1], 1)
+
     prev_scale = jnp.where(has_prev, stiffness, 0.0).astype(F32)
     next_scale = jnp.where(has_next, stiffness, 0.0).astype(F32)
     for t, rows in enumerate(tiles):
@@ -169,21 +212,18 @@
                 left = dot(pm_ref[out, rows], block)
                 image_ref[out, :] = image_ref[out, :] - prev_scale * left
     block = behind_ref[tiles[-1], :]
-    gram = None
+    curvature = None
     for t, out in enumerate(tiles):
         left = dot(pm_ref[out, tiles[-1]], block)
         index = lax.broadcasted_iota(jnp.int32, (step, breadth), 0) + t * step
         image = jnp.where(index < size, image_ref[out, :] - prev_scale * left, 0.0)
         image_ref[out, :] = image
-        lhs = jnp.concatenate([rounded_ref[out, :].astype(F32), image], axis=1)
-        rhs = jnp.concatenate([image, live_ref[out, :]], axis=1)
-        term = dot(lhs, rhs, ((0,), (0,)), HIGHEST)
-        gram = term if gram is None else gram + term
-    curvature = gram[:breadth, :breadth]
-    others = (gram[:breadth, breadth:], gram[breadth:, :breadth], gram[breadth:, breadth:])
+        term = dot(rounded_ref[out, :], jnp.concatenate(two_parts(image), axis=1), ((0,), (0,)))
+        curvature = term if curvature is None else curvature + term
+    curvature = curvature[:, :breadth] + curvature[:, breadth:]
     slab = breadth // nsub
-    for s in range(nsub):
-        cgram_ref[s] = curvature[s * slab : (s + 1) * slab, :]
+    half = breadth // 2
+    pack(curvature, cgram_ref)
 
     sent = forward + backward
 
@@ -219,6 +259,17 @@
         return total
 
     cx = scatter(cgram_ref, sub, nsub, cxin_ref, cxs, cxr, sub_ids)
+    gram = None
+    for out in tiles:
+        ih, im = two_parts(image_ref[out, :])
+        lh, lm = two_parts(live_ref[out, :])
+        lhs = jnp.concatenate([rounded_ref[out, :], ih, im], axis=1)
+        rhs = jnp.concatenate([lh, ih, lm, im], axis=1)
+        term = dot(lhs, rhs, ((0,), (0,)))
+        gram = term if gram is None else gram + term
+    first = gram[: 2 * breadth, : 2 * breadth] + gram[: 2 * breadth, 2 * breadth :]
+    second = first[breadth:, :] + gram[2 * breadth :, : 2 * breadth]
+    others = (first[:breadth, :breadth], second[:, breadth:], second[:, :breadth])
     for s in range(nsub):
         for k, piece in enumerate(others):
             gram_ref[s, k * slab : (k + 1) * slab, :] = piece[s * slab : (s + 1) * slab, :]
@@ -244,10 +295,10 @@
 
     for copy in cx2:
         copy.wait_recv()
-    summed = jnp.concatenate([csum_ref[s] for s in range(nsub)], axis=0)
+    summed = unpack(csum_ref)
     rows = lax.broadcasted_iota(jnp.int32, (breadth, breadth), 0)
     lanes = lax.broadcasted_iota(jnp.int32, (breadth, breadth), 1)
-    inverse_ref[...] = 0.5 * (summed + summed.T) + jnp.where(rows == lanes, 1.0 - keep, 0.0)
+    inverse_ref[...] = summed + jnp.where(rows == lanes, 1.0 - keep, 0.0)
 
     def sweep(first, last):
         def one(k, carry):
@@ -270,11 +321,17 @@
         copy.wait_send()
 
 
+def hbm_only(array):
+    return pltpu.with_memory_space_constraint(array, pltpu.HBM)
+
+
 def communicate(operator, rhs, sizes, neighbours, kept, ny, nz, nx, nc):
     height, breadth = rhs.shape[1:]
     nsub = nx * nc
     slab = breadth // nsub
     piece = 3 * slab // ny
+    packed = slab // 2 + 1
+    signals = pltpu.SemaphoreType.REGULAR
     vmem = pl.BlockSpec(memory_space=pltpu.VMEM)
     hbm = pl.BlockSpec(memory_space=pltpu.HBM)
     dma = pltpu.SemaphoreType.DMA
@@ -284,12 +341,13 @@
         name="exchange_and_sums",
         out_shape=(
             jax.ShapeDtypeStruct(tall, F32),
+            jax.ShapeDtypeStruct(tall, BF16),
             jax.ShapeDtypeStruct(tall, F32),
             jax.ShapeDtypeStruct((breadth, breadth), F32),
             jax.ShapeDtypeStruct((nsub, 3 * slab, breadth), F32),
         ),
         in_specs=[hbm, hbm, pl.BlockSpec(memory_space=pltpu.SMEM), hbm, hbm],
-        out_specs=(vmem,) * 4,
+        out_specs=(vmem,) * 5,
         scratch_shapes=[
             pltpu.VMEM((height, height), BF16),
             pltpu.VMEM((height, height), BF16),
@@ -297,16 +355,15 @@
             pltpu.VMEM(tall, BF16),
             pltpu.VMEM(tall, BF16),
             pltpu.VMEM(tall, BF16),
-            pltpu.VMEM(tall, BF16),
             pltpu.VMEM((1, height), jnp.int32),
             pltpu.VMEM((1, breadth), jnp.int32),
-            pltpu.VMEM((nsub, slab, breadth), F32),
-            pltpu.VMEM((nsub, slab, breadth), F32),
-            pltpu.VMEM((slab, breadth), F32),
-            pltpu.VMEM((ny, slab, breadth), F32),
-            pltpu.VMEM((slab, breadth), F32),
-            pltpu.VMEM((nz, slab, breadth), F32),
-            pltpu.VMEM((nsub, slab, breadth), F32),
+            pltpu.VMEM((nsub, packed, breadth), F32),
+            pltpu.VMEM((nsub, packed, breadth), F32),
+            pltpu.VMEM((packed, breadth), F32),
+            pltpu.VMEM((ny, packed, breadth), F32),
+            pltpu.VMEM((packed, breadth), F32),
+            pltpu.VMEM((nz, packed, breadth), F32),
+            pltpu.VMEM((nsub, packed, breadth), F32),
             pltpu.VMEM((nsub, 3 * slab, breadth), F32),
             pltpu.VMEM((nsub, 3 * slab, breadth), F32),
             pltpu.VMEM((ny, piece, breadth), F32),
@@ -314,6 +371,7 @@
             pltpu.VMEM((piece, breadth), F32),
             pltpu.VMEM((nz, piece, breadth), F32),
             pltpu.VMEM((ny, piece, breadth), F32),
+            signals((max(ny - 2, 2),)), signals((max(nz - 2, 2),)),
             dma((4,)),
             dma((CHUNKS,)), dma((CHUNKS,)), dma((CHUNKS,)), dma((CHUNKS,)),
             dma((nsub,)), dma((nsub,)), dma((ny,)), dma((ny,)), dma((nz,)), dma((nz,)), dma((nsub,)), dma((nsub,)),
@@ -321,22 +379,21 @@
             dma((ny,)), dma((ny,)), dma((nsub,)), dma((nsub,)),
         ],
         compiler_params=pltpu.CompilerParams(
-            collective_id=0, has_side_effects=True, vmem_limit_bytes=55230000
+            collective_id=0, has_side_effects=True, vmem_limit_bytes=40 * 2**20
         ),
-    )(operator, rhs, sizes, neighbours, kept)
-
-
-BLOCK = 8
+    )(hbm_only(operator), hbm_only(rhs), sizes, hbm_only(neighbours), hbm_only(kept))
+
+
+BLOCK = 16
 
 
 def update_kernel(
-    live_ref, image_ref, inverse_ref, rest_ref, keep_ref,
+    live_ref, rounded_ref, image_ref, inverse_ref, rest_ref,
     solution_hbm, residual_hbm, direction_hbm,
     solution_ref, residual_ref, direction_ref, sems,
 ):
     nsub, rows3 = rest_ref.shape[:2]
     slab = rows3 // 3
-    keep = keep_ref[...].astype(F32)
     height = live_ref.shape[0]
     step = height // CHUNKS
 
@@ -355,8 +412,7 @@
     for t in range(CHUNKS):
         rows = pl.ds(t * step, step)
         live = live_ref[rows, :]
-        rounded = (live * keep).astype(BF16)
-        spread = dot(rounded, wide)
+        spread = dot(rounded_ref[rows, :], wide)
         ih, im, il = three_parts(image_ref[rows, :])
         first = dot(ih, wide[:, : 3 * n])
         second = dot(im, wide[:, : 2 * n])
@@ -377,7 +433,7 @@
         copy.wait()
 
 
-def update(live, image, inverse, rest, kept):
+def update(live, rounded, image, inverse, rest):
     vmem = pl.BlockSpec(memory_space=pltpu.VMEM)
     return pl.pallas_call(
         update_kernel,
@@ -387,12 +443,12 @@
         out_specs=[pl.BlockSpec(memory_space=pltpu.HBM)] * 3,
         scratch_shapes=[pltpu.VMEM(live.shape, F32)] * 3 + [pltpu.SemaphoreType.DMA((3, CHUNKS))],
         compiler_params=pltpu.CompilerParams(vmem_limit_bytes=40 * 2**20),
-    )(live, image, inverse, rest, kept)
+    )(live, rounded, image, inverse, rest)
 
 
 def per_device(ny, nz, nx, nc, operator, rhs, interface_sizes, neighbour_rows, kept_columns):
     results = communicate(operator, rhs, interface_sizes, neighbour_rows, kept_columns, ny, nz, nx, nc)
-    return tuple(update(*results, kept_columns))
+    return tuple(update(*results))
 
 
 def solution(mesh, grid=(8, 12, 4, 2)):

time: 63.3 us -> 58.4 us (0.923)
  Pallas kernels: 60.4 us -> 56.9 us
  local copies, waits for them, and re-layouts: 1.33 us -> 0 us
    pallas_call x1, Pallas kernels: 58 us -> 54.5 us  [communicate(): pl.pallas_call(functools.partial(comm_kernel, ny, nz, nx, nc), name='exch...]
    unnamed x4 -> x0, local copies, waits for them, and re-layouts: 1.33 us -> none
where the time goes in v3:
time: 58.4 us; the launch traced here: 58.2 us
  Pallas kernels  56.9 us (97%)
  between operations  1.28 us (2%)
    pallas_call x1, Pallas kernels, communicate(): pl.pallas_call(functools.partial(comm_kernel, ny, nz, nx, nc), name='exch...  54.5 us
    pallas_call x1, Pallas kernels, update(): pl.pallas_call(update_kernel, name='update', out_shape=[jax.ShapeDtypeStr...  2.41 us

profile of v3, /device:TPU:1, one launch (start us, length us, event | category | flops | bytes accessed | tf_op | source)
XLA Modules:
  0.0 58.2 jit_solution(15915274610108483818)
XLA Ops:
  1.3 54.5 %exchange_and_sums.1 = (f32[1024,128]{1,0:T(8,128)S(1)}, bf16[1024,128]{1,0:T(8,128)(2,1)S(1)}, f32[1024,128]{1,0:T(8,128)S(1)}, f32[128,128]{1,0:T(8,128)S(1)}, f32[8,48,128]{2,1,0:T(8,128)S(1)}) custom-call(bf16[1,1024,1024]{2,1,0:T(8,128)(2,1)} %op_hbm.1, f32[1,1024,128]{2,1,0:T(8,128)} %rhs_hbm.1, s32[1]{0:T(128)S(6)} %copy.8.size_ref, ...), custom_call_target="tpu_custom_call" | custom-call | tf_op jit(solution)/shard_map/exchange_and_sums/pallas_call | solution.py:339
  55.8 2.4 %update.1 = (f32[1,1024,128]{2,1,0:T(8,128)}, f32[1,1024,128]{2,1,0:T(8,128)}, f32[1,1024,128]{2,1,0:T(8,128)}) custom-call(f32[1024,128]{1,0:T(8,128)S(1)} %get-tuple-element.8.live_ref, bf16[1024,128]{1,0:T(8,128)(2,1)S(1)} %get-tuple-element.9.rounded_ref, f32[1024,128]{1,0:T(8,128)S(1)} %get-tuple-element.10.image_ref, ...), custom_call_target="tpu_custom_call" | custom-call | tf_op jit(solution)/shard_map/update/pallas_call | solution.py:438

commit v4 on v3

--- a/solution.py
+++ b/solution.py
@@ -225,36 +225,32 @@
     half = breadth // 2
     pack(curvature, cgram_ref)
 
-    sent = forward + backward
+    sent = []
+
+    def whole(sources, landings, count, send, recv, ids):
+        sent.append(remote(sources, sources, send, recv, ids[1]))
+        return remote(landings, landings, send, recv, ids[1])
 
     def scatter(source, place, count, landing, send, recv, ids):
-        copies = []
         for d in range(1, count):
-            peer = lax.rem(place + d, count)
-            copies.append(remote(source.at[peer], landing.at[d], send.at[d], recv.at[d], ids[d]))
-            copies[-1].start()
-        sent.extend(copies)
-        return copies
+            remote(source.at[lax.rem(place + d, count)], landing.at[d], send, recv, ids[d]).start()
+        return whole(source.at[pl.ds(0, count - 1)], landing.at[pl.ds(1, count - 1)], count, send, recv, ids)
 
     def spread(source, count, landing, send, recv, ids):
-        copies = []
         for d in range(1, count):
-            copies.append(remote(source, landing.at[d], send.at[d], recv.at[d], ids[d]))
-            copies[-1].start()
-        sent.extend(copies)
-        return copies
+            remote(source, landing.at[d], send, recv, ids[d]).start()
+        slots = landing.at[pl.ds(1, count - 1)]
+        return whole(slots, slots, count, send, recv, ids)
 
     def share(array, place, count, send, recv, ids):
-        copies = []
         for d in range(1, count):
-            copies.append(remote(array.at[place], array.at[place], send.at[d], recv.at[d], ids[d]))
-            copies[-1].start()
-        sent.extend(copies)
-        return copies
+            remote(array.at[place], array.at[place], send, recv, ids[d]).start()
+        slots = array.at[pl.ds(0, count - 1)]
+        return whole(slots, slots, count, send, recv, ids)
 
     def add_up(total, copies, landing):
-        for d, copy in enumerate(copies, 1):
-            copy.wait_recv()
+        copies.wait_recv()
+        for d in range(1, landing.shape[0]):
             total = total + landing[d]
         return total
 
@@ -293,8 +289,11 @@
     part_ref[y] = add_up(zown_ref[...], rz, zin_ref)
     ry2 = share(part_ref, y, ny, ys2, yr2, y_ids)
 
-    for copy in cx2:
-        copy.wait_recv()
+    cx2.wait_recv()
+    ry2.wait_recv()
+    for v in range(ny):
+        rest_ref[sub, v * rows_y : (v + 1) * rows_y, :] = part_ref[v]
+    rx2 = share(rest_ref, sub, nsub, xs2, xr2, sub_ids)
     summed = unpack(csum_ref)
     rows = lax.broadcasted_iota(jnp.int32, (breadth, breadth), 0)
     lanes = lax.broadcasted_iota(jnp.int32, (breadth, breadth), 1)
@@ -308,17 +307,10 @@
         lax.fori_loop(first, last, one, 0)
 
     blocks = breadth // BLOCK
-    sweep(0, blocks // 4)
-    for copy in ry2:
-        copy.wait_recv()
-    for v in range(ny):
-        rest_ref[sub, v * rows_y : (v + 1) * rows_y, :] = part_ref[v]
-    rx2 = share(rest_ref, sub, nsub, xs2, xr2, sub_ids)
-    sweep(blocks // 4, blocks)
-    for copy in rx2:
-        copy.wait_recv()
-    for copy in sent:
+    sweep(0, blocks)
+    for copy in forward + backward + sent:
         copy.wait_send()
+    rx2.wait_recv()
 
 
 def hbm_only(array):
@@ -374,9 +366,7 @@
             signals((max(ny - 2, 2),)), signals((max(nz - 2, 2),)),
             dma((4,)),
             dma((CHUNKS,)), dma((CHUNKS,)), dma((CHUNKS,)), dma((CHUNKS,)),
-            dma((nsub,)), dma((nsub,)), dma((ny,)), dma((ny,)), dma((nz,)), dma((nz,)), dma((nsub,)), dma((nsub,)),
-            dma((nsub,)), dma((nsub,)), dma((ny,)), dma((ny,)), dma((nz,)), dma((nz,)),
-            dma((ny,)), dma((ny,)), dma((nsub,)), dma((nsub,)),
+            *[dma(())] * 18,
         ],
         compiler_params=pltpu.CompilerParams(
             collective_id=0, has_side_effects=True, vmem_limit_bytes=40 * 2**20

time: 58.4 us -> 56 us (0.959)
  Pallas kernels: 56.9 us -> 54.6 us
    pallas_call x1, Pallas kernels: 54.5 us -> 52.2 us  [communicate(): pl.pallas_call(functools.partial(comm_kernel, ny, nz, nx, nc), name='exch...]
where the time goes in v4:
time: 56 us; the launch traced here: 55.9 us
  Pallas kernels  54.6 us (98%)
  between operations  1.28 us (2%)
    pallas_call x1, Pallas kernels, communicate(): pl.pallas_call(functools.partial(comm_kernel, ny, nz, nx, nc), name='exch...  52.2 us
    pallas_call x1, Pallas kernels, update(): pl.pallas_call(update_kernel, name='update', out_shape=[jax.ShapeDtypeStr...  2.42 us

profile of v4, /device:TPU:1, one launch (start us, length us, event | category | flops | bytes accessed | tf_op | source)
XLA Modules:
  0.0 55.9 jit_solution(2681801458093696954)
XLA Ops:
  1.3 52.2 %exchange_and_sums.1 = (f32[1024,128]{1,0:T(8,128)S(1)}, bf16[1024,128]{1,0:T(8,128)(2,1)S(1)}, f32[1024,128]{1,0:T(8,128)S(1)}, f32[128,128]{1,0:T(8,128)S(1)}, f32[8,48,128]{2,1,0:T(8,128)S(1)}) custom-call(bf16[1,1024,1024]{2,1,0:T(8,128)(2,1)} %op_hbm.1, f32[1,1024,128]{2,1,0:T(8,128)} %rhs_hbm.1, s32[1]{0:T(128)S(6)} %copy.8.size_ref, ...), custom_call_target="tpu_custom_call" | custom-call | tf_op jit(solution)/shard_map/exchange_and_sums/pallas_call | solution.py:331
  53.5 2.4 %update.1 = (f32[1,1024,128]{2,1,0:T(8,128)}, f32[1,1024,128]{2,1,0:T(8,128)}, f32[1,1024,128]{2,1,0:T(8,128)}) custom-call(f32[1024,128]{1,0:T(8,128)S(1)} %get-tuple-element.8.live_ref, bf16[1024,128]{1,0:T(8,128)(2,1)S(1)} %get-tuple-element.9.rounded_ref, f32[1024,128]{1,0:T(8,128)S(1)} %get-tuple-element.10.image_ref, ...), custom_call_target="tpu_custom_call" | custom-call | tf_op jit(solution)/shard_map/update/pallas_call | solution.py:428

commit v5 on v4

--- a/solution.py
+++ b/solution.py
@@ -96,6 +96,10 @@
     lower = jnp.where(lane > row, packed, jnp.where(lane == row, diagonal, turned[:half, :]))
     lower = jnp.where(lane < half, turned[half:, :], pltpu.roll(lower, half, axis=1))
     return jnp.concatenate([upper, lower], axis=0)
+
+
+def far_first(count):
+    return sorted(range(1, count), key=lambda d: -min(d, count - d))
 
 
 def comm_kernel(
@@ -232,18 +236,18 @@
         return remote(landings, landings, send, recv, ids[1])
 
     def scatter(source, place, count, landing, send, recv, ids):
-        for d in range(1, count):
+        for d in far_first(count):
             remote(source.at[lax.rem(place + d, count)], landing.at[d], send, recv, ids[d]).start()
         return whole(source.at[pl.ds(0, count - 1)], landing.at[pl.ds(1, count - 1)], count, send, recv, ids)
 
     def spread(source, count, landing, send, recv, ids):
-        for d in range(1, count):
+        for d in far_first(count):
             remote(source, landing.at[d], send, recv, ids[d]).start()
         slots = landing.at[pl.ds(1, count - 1)]
         return whole(slots, slots, count, send, recv, ids)
 
     def share(array, place, count, send, recv, ids):
-        for d in range(1, count):
+        for d in far_first(count):
             remote(array.at[place], array.at[place], send, recv, ids[d]).start()
         slots = array.at[pl.ds(0, count - 1)]
         return whole(slots, slots, count, send, recv, ids)

time: 56 us -> 55 us (0.982)
  Pallas kernels: 54.6 us -> 53.6 us
    pallas_call x1, Pallas kernels: 52.2 us -> 51.1 us  [communicate(): pl.pallas_call(functools.partial(comm_kernel, ny, nz, nx, nc), name='exch...]
where the time goes in v5:
time: 55 us; the launch traced here: 54.8 us
  Pallas kernels  53.6 us (97%)
  between operations  1.28 us (2%)
    pallas_call x1, Pallas kernels, communicate(): pl.pallas_call(functools.partial(comm_kernel, ny, nz, nx, nc), name='exch...  51.1 us
    pallas_call x1, Pallas kernels, update(): pl.pallas_call(update_kernel, name='update', out_shape=[jax.ShapeDtypeStr...  2.41 us

profile of v5, /device:TPU:1, one launch (start us, length us, event | category | flops | bytes accessed | tf_op | source)
XLA Modules:
  0.0 54.8 jit_solution(16766757536177490165)
XLA Ops:
  1.3 51.1 %exchange_and_sums.1 = (f32[1024,128]{1,0:T(8,128)S(1)}, bf16[1024,128]{1,0:T(8,128)(2,1)S(1)}, f32[1024,128]{1,0:T(8,128)S(1)}, f32[128,128]{1,0:T(8,128)S(1)}, f32[8,48,128]{2,1,0:T(8,128)S(1)}) custom-call(bf16[1,1024,1024]{2,1,0:T(8,128)(2,1)} %op_hbm.1, f32[1,1024,128]{2,1,0:T(8,128)} %rhs_hbm.1, s32[1]{0:T(128)S(6)} %copy.8.size_ref, ...), custom_call_target="tpu_custom_call" | custom-call | tf_op jit(solution)/shard_map/exchange_and_sums/pallas_call | solution.py:335
  52.4 2.4 %update.1 = (f32[1,1024,128]{2,1,0:T(8,128)}, f32[1,1024,128]{2,1,0:T(8,128)}, f32[1,1024,128]{2,1,0:T(8,128)}) custom-call(f32[1024,128]{1,0:T(8,128)S(1)} %get-tuple-element.8.live_ref, bf16[1024,128]{1,0:T(8,128)(2,1)S(1)} %get-tuple-element.9.rounded_ref, f32[1024,128]{1,0:T(8,128)S(1)} %get-tuple-element.10.image_ref, ...), custom_call_target="tpu_custom_call" | custom-call | tf_op jit(solution)/shard_map/update/pallas_call | solution.py:432

commit v6 on v5

--- a/solution.py
+++ b/solution.py
@@ -36,13 +36,13 @@
 def sweep_block(k, ref):
     n = ref.shape[0]
     b = BLOCK
-    start = pl.multiple_of(k * b, b)
+    start = k * b
     lane = lax.broadcasted_iota(jnp.int32, (b, n), 1)
     row = lax.broadcasted_iota(jnp.int32, (b, n), 0)
     wide_lane = lax.broadcasted_iota(jnp.int32, (n, n), 1)
     panel = ref[pl.ds(start, b), :]
-    turned = pltpu.roll(panel, lax.rem(n - start, n), axis=1)
-    columns = [jnp.broadcast_to(turned[:, j : j + 1], (b, n)) for j in range(b)]
+    turned = panel
+    columns = [jnp.broadcast_to(turned[:, start + j : start + j + 1], (b, n)) for j in range(b)]
     inside = (lane >= start) & (lane < start + b)
     work = jnp.where(inside, jnp.where(lane - start == row, 1.0, 0.0), panel)
     for j in range(b):
@@ -308,7 +308,8 @@
             sweep_block(k, inverse_ref)
             return carry
 
-        lax.fori_loop(first, last, one, 0)
+        for k in range(first, last):
+            one(k, 0)
 
     blocks = breadth // BLOCK
     sweep(0, blocks)

time: 55 us -> 55 us (level)
  no operation moved by 1% of the time
where the time goes in v6:
time: 55 us; the launch traced here: 54.9 us
  Pallas kernels  53.6 us (97%)
  between operations  1.28 us (2%)
    pallas_call x1, Pallas kernels, communicate(): pl.pallas_call(functools.partial(comm_kernel, ny, nz, nx, nc), name='exch...  51.2 us
    pallas_call x1, Pallas kernels, update(): pl.pallas_call(update_kernel, name='update', out_shape=[jax.ShapeDtypeStr...  2.41 us

profile of v6, /device:TPU:1, one launch (start us, length us, event | category | flops | bytes accessed | tf_op | source)
XLA Modules:
  0.0 54.9 jit_solution(1191196507931394052)
XLA Ops:
  1.3 51.2 %exchange_and_sums.1 = (f32[1024,128]{1,0:T(8,128)S(1)}, bf16[1024,128]{1,0:T(8,128)(2,1)S(1)}, f32[1024,128]{1,0:T(8,128)S(1)}, f32[128,128]{1,0:T(8,128)S(1)}, f32[8,48,128]{2,1,0:T(8,128)S(1)}) custom-call(bf16[1,1024,1024]{2,1,0:T(8,128)(2,1)} %op_hbm.1, f32[1,1024,128]{2,1,0:T(8,128)} %rhs_hbm.1, s32[1]{0:T(128)S(6)} %copy.8.size_ref, ...), custom_call_target="tpu_custom_call" | custom-call | tf_op jit(solution)/shard_map/exchange_and_sums/pallas_call | solution.py:336
  52.4 2.4 %update.1 = (f32[1,1024,128]{2,1,0:T(8,128)}, f32[1,1024,128]{2,1,0:T(8,128)}, f32[1,1024,128]{2,1,0:T(8,128)}) custom-call(f32[1024,128]{1,0:T(8,128)S(1)} %get-tuple-element.8.live_ref, bf16[1024,128]{1,0:T(8,128)(2,1)S(1)} %get-tuple-element.9.rounded_ref, f32[1024,128]{1,0:T(8,128)S(1)} %get-tuple-element.10.image_ref, ...), custom_call_target="tpu_custom_call" | custom-call | tf_op jit(solution)/shard_map/update/pallas_call | solution.py:433
